TPU v7x, 128 devices: a whole 4x4x4 slice. The times are simulated.
128 devices in a mesh: ray: 16 (over x, z), tile: 8 (over y, core).
Axes of the slice: x: 4, y: 4, z: 4, core: 2. Of those that a mesh axis runs over, the one named last changes fastest.
Arguments:
- data: float32 [64, 262144], P(None, ('ray', 'tile')), may hold values from -6 to 6
- sensitivity: bfloat16 [4096, 256, 512], P(('ray', 'tile')), may hold values from -0.25 to 0.25
- block_tiles: int32 [128, 8, 4], P(('ray', 'tile')), may hold values from 0 to 47
- block_bundles: int32 [128, 8, 4], P(('ray', 'tile')), may hold values from 0 to 7
Outputs:
- solution: float32 [64, 196608], P(None, 'tile')
- residual: float32 [64, 262144], P(None, ('ray', 'tile'))
Inputs may be any that keep to these rules, and one draw needn't show every extreme that they name: `block_tiles`: position of the block's tile among the 48 tiles of the owner given by the second index. `block_bundles`: the block's ray bundle among the device's 8 bundles.
All inputs are finite; a program needn't handle non-finite values.
Results may differ from a plain program's by a relative error of at most 0.004.
The roundings to bfloat16 on the way count: a program that leaves them out, or rounds other values in their place, can miss the bound.
Values may be sent and summed in bfloat16 or wider, within the bound.
A program may use at most 128 MiB of HBM per device.

v0:
```python
import jax
import jax.numpy as jnp
from jax import lax
from jax.sharding import PartitionSpec as P

RB = 256
CB = 512
ITERS = 2
BUND_DEV = 8
TILE_DEV = 48
eps_norm = 1e-06


def per_device(data, sensitivity, block_tiles, block_bundles):
    columns = data.shape[0]
    bundles = block_bundles.reshape(-1)
    requests = lax.all_to_all(block_tiles, "tile", split_axis=1, concat_axis=1, tiled=True).reshape(
        -1
    )
    bundle_onehot = (bundles[:, None] == jnp.arange(BUND_DEV, dtype=jnp.int32)[None, :]).astype(
        jnp.float32
    )
    owner_onehot = (requests[:, None] == jnp.arange(TILE_DEV, dtype=jnp.int32)[None, :]).astype(
        jnp.bfloat16
    )

    def fetch(field_bf):
        owned = field_bf.reshape(columns, TILE_DEV, CB)
        outgoing = jnp.take(owned, requests, axis=1)
        tiles = lax.all_to_all(outgoing, "tile", split_axis=1, concat_axis=1, tiled=True)
        return tiles

    def forward(field_bf):
        tiles = fetch(field_bf)
        partial_value = jnp.einsum(
            "cnk,nrk->ncr", tiles, sensitivity, preferred_element_type=jnp.float32
        )
        summed = jnp.einsum(
            "ncr,nb->cbr", partial_value, bundle_onehot, precision=lax.Precision.HIGHEST
        )
        return summed.reshape(columns, BUND_DEV * RB)

    def adjoint(rays_bf):
        picked = jnp.take(rays_bf.reshape(columns, BUND_DEV, RB), bundles, axis=1)
        terms = jnp.einsum(
            "cnr,nrk->cnk", picked, sensitivity, preferred_element_type=jnp.float32
        ).astype(jnp.bfloat16)
        arrived = lax.all_to_all(terms, "tile", split_axis=1, concat_axis=1, tiled=True)
        owned = jnp.einsum(
            "cnk,nt->ctk", arrived, owner_onehot, preferred_element_type=jnp.float32
        ).reshape(columns, TILE_DEV * CB)
        total = lax.psum(owned, "ray")
        return total

    def cell_norm(field):
        local = jnp.sum(field * field, axis=1)
        total = lax.psum(local, "tile")
        return jnp.sqrt(total + eps_norm)

    def ray_norm(rays):
        total = lax.psum(jnp.sum(rays * rays, axis=1), ("ray", "tile"))
        return jnp.sqrt(total + eps_norm)

    beta_now = ray_norm(data)
    rays_dir = data / beta_now[:, None]
    model_dir = adjoint(rays_dir.astype(jnp.bfloat16))
    alpha_now = cell_norm(model_dir)
    model_dir = model_dir / alpha_now[:, None]
    search = model_dir
    solution = jnp.zeros_like(model_dir)
    phi_bar = beta_now
    rho_bar = alpha_now
    for step in range(ITERS):
        rounded = model_dir.astype(jnp.bfloat16)
        rays_dir = forward(rounded) - alpha_now[:, None] * rays_dir
        beta_now = ray_norm(rays_dir)
        rays_dir = rays_dir / beta_now[:, None]
        rho_now = jnp.sqrt(rho_bar * rho_bar + beta_now * beta_now)
        cosine = rho_bar / rho_now
        sine_part = beta_now / rho_now
        phi_now = cosine * phi_bar
        phi_bar = sine_part * phi_bar
        solution = solution + (phi_now / rho_now)[:, None] * search
        if step + 1 < ITERS:
            model_dir = adjoint(rays_dir.astype(jnp.bfloat16)) - beta_now[:, None] * model_dir
            alpha_now = cell_norm(model_dir)
            model_dir = model_dir / alpha_now[:, None]
            theta_now = sine_part * alpha_now
            rho_bar = -cosine * alpha_now
            search = model_dir - (theta_now / rho_now)[:, None] * search
    residual = data - forward(solution.astype(jnp.bfloat16))
    return (solution, residual)


def solution(mesh):
    return jax.shard_map(
        per_device,
        mesh=mesh,
        in_specs=(
            P(None, ("ray", "tile")),
            P(("ray", "tile"), None, None),
            P(("ray", "tile"), None, None),
            P(("ray", "tile"), None, None),
        ),
        out_specs=(P(None, "tile"), P(None, ("ray", "tile"))),
        check_vma=False,
    )
```

profile of v0, /device:TPU:1, one launch (start us, length us, event | category | flops | bytes accessed | tf_op | source)
XLA Modules:
  0.0 731.6 jit_solution(17410393598439722855)
XLA Ops:
  8.5 6.0 all-to-all-start
  16.5 67.7 %psum.49 = f32[64]{0:T(128)S(1)} all-reduce(f32[64]{0:T(128)S(1)} %multiply_reduce_fusion.4), channel_id=1, replica_groups=mesh['ray'=16,'tile'=8] {'ray','tile'}, use_global_device_ids=true, to_apply=%region_1.0 | all-reduce | flops 64 | bytes 512 | tf_op jit(solution)/shard_map/psum | solution.py:61
  86.1 6.3 convert_bitcast_fusion.1
  92.4 4.4 all-to-all-start.1
  98.1 25.1 %all-to-all-done.1 = bf16[64,32,512]{2,0,1:T(8,128)(2,1)S(1)} async-done(((bf16[64,32,512]{2,0,1:T(8,128)(2,1)}), bf16[64,32,512]{2,0,1:T(8,128)(2,1)S(1)}, u32[]{:S(2)}, u32[]{:S(2)}) %all-to-all-start.1) | async-done | bytes 2097184 | tf_op jit(solution)/shard_map/all_to_all | solution.py:48
  124.9 6.3 copy.39
  131.3 119.1 %all-reduce.3.cloned.1.call-done = f32[64,24576]{1,0:T(8,128)} async-done(((f32[64,24576]{1,0:T(8,128)}), f32[64,24576]{1,0:T(8,128)}) %all-reduce.3.cloned.1.call-update) | async-done | bytes 6291472 | tf_op jit(solution)/shard_map/psum | solution.py:52
  253.7 12.4 %psum.51 = f32[64]{0:T(128)S(1)} all-reduce(f32[64]{0:T(128)S(1)} %multiply_reduce_fusion.1), channel_id=1, replica_groups=mesh['ray'=16,'tile'=8] {'tile'}, use_global_device_ids=true, to_apply=%region_4.6 | all-reduce | flops 64 | bytes 512 | tf_op jit(solution)/shard_map/psum | solution.py:57
  273.7 31.7 %all_to_all.30 = bf16[64,32,512]{2,0,1:T(8,128)(2,1)S(1)} all-to-all(bf16[64,32,512]{2,0,1:T(8,128)(2,1)S(1)} %select_bitcast_fusion.2), channel_id=1, replica_groups=mesh['ray'=16,'tile'=8] {'tile'}, dimensions={1} | all-to-all | bytes 4194304 | tf_op jit(solution)/shard_map/all_to_all | solution.py:30
  305.4 6.0 fusion.41
  313.9 64.5 %psum.52 = f32[64]{0:T(128)S(1)} all-reduce(f32[64]{0:T(128)S(1)} %get-tuple-element.11), channel_id=1, replica_groups=mesh['ray'=16,'tile'=8] {'ray','tile'}, use_global_device_ids=true, to_apply=%region_6.0 | all-reduce | flops 64 | bytes 512 | tf_op jit(solution)/shard_map/psum | solution.py:61
  379.2 5.0 convert_bitcast_fusion
  384.2 30.1 %all_to_all.31 = bf16[64,32,512]{2,0,1:T(8,128)(2,1)S(1)} all-to-all(bf16[64,32,512]{2,0,1:T(8,128)(2,1)S(1)} %convert_bitcast_fusion), channel_id=1, replica_groups=mesh['ray'=16,'tile'=8] {'tile'}, dimensions={1} | all-to-all | bytes 4194304 | tf_op jit(solution)/shard_map/all_to_all | solution.py:48
  416.0 6.3 copy.41
  422.3 118.9 %all-reduce.5.cloned.1.call-done = f32[64,24576]{1,0:T(8,128)} async-done(((f32[64,24576]{1,0:T(8,128)}), f32[64,24576]{1,0:T(8,128)}) %all-reduce.5.cloned.1.call-update) | async-done | bytes 6291472 | tf_op jit(solution)/shard_map/psum | solution.py:52
  541.2 5.8 multiply_reduce_fusion
  547.0 12.4 %psum.54 = f32[64]{0:T(128)S(1)} all-reduce(f32[64]{0:T(128)S(1)} %multiply_reduce_fusion), channel_id=1, replica_groups=mesh['ray'=16,'tile'=8] {'tile'}, use_global_device_ids=true, to_apply=%region_9.12 | all-reduce | flops 64 | bytes 512 | tf_op jit(solution)/shard_map/psum | solution.py:57
  559.4 5.2 fusion.10
  568.9 31.7 %all_to_all.32 = bf16[64,32,512]{2,0,1:T(8,128)(2,1)S(1)} all-to-all(bf16[64,32,512]{2,0,1:T(8,128)(2,1)S(1)} %select_bitcast_fusion.1), channel_id=1, replica_groups=mesh['ray'=16,'tile'=8] {'tile'}, dimensions={1} | all-to-all | bytes 4194304 | tf_op jit(solution)/shard_map/all_to_all | solution.py:30
  600.7 6.0 fusion.42
  609.1 64.8 %psum.55 = f32[64]{0:T(128)S(1)} all-reduce(f32[64]{0:T(128)S(1)} %multiply_reduce_fusion.2), channel_id=1, replica_groups=mesh['ray'=16,'tile'=8] {'ray','tile'}, use_global_device_ids=true, to_apply=%region_11.14 | all-reduce | flops 64 | bytes 512 | tf_op jit(solution)/shard_map/psum | solution.py:61
  673.9 7.4 %fusion.38 = (bf16[64,24576]{1,0:T(8,128)(2,1)S(1)}, f32[64,24576]{1,0:T(8,128)}) fusion(f32[64]{0:T(128)S(1)} %multiply_divide_fusion, f32[64]{0:T(128)S(1)} %add_sqrt_fusion, f32[64,24576]{1,0:T(8,128)} %all-reduce.5.cloned.1.call-done, f32[64]{0:T(128)S(1)} %get-tuple-element.13, f32[64]{0:T(128)S(1)} %get-tuple-element.9, ...), kind=kLoop, calls=%fused_computation.76 | loop fusion | flops 15728640 | bytes 22021632 | tf_op jit(solution)/shard_map/convert_element_type | solution.py:91
  685.6 30.1 %all_to_all.33 = bf16[64,32,512]{2,0,1:T(8,128)(2,1)S(1)} all-to-all(bf16[64,32,512]{2,0,1:T(8,128)(2,1)S(1)} %select_bitcast_fusion), channel_id=1, replica_groups=mesh['ray'=16,'tile'=8] {'tile'}, dimensions={1} | all-to-all | bytes 4194304 | tf_op jit(solution)/shard_map/all_to_all | solution.py:30
  715.7 6.0 fusion.43
  (60 shorter events, 37.9 us)
Async XLA Ops:
  8.5 83.9 %all-to-all-start = ((s32[1,8,4]{2,0,1:T(1,128)}), s32[1,8,4]{2,0,1:T(1,128)S(1)}, u32[]{:S(2)}, u32[]{:S(2)}) async-start(s32[1,8,4]{2,0,1:T(1,128)} %copy.22), calls=%async_computation | async-start | bytes 8192 | tf_op jit(solution)/shard_map/all_to_all | solution.py:17
  92.4 30.8 %all-to-all-start.1 = ((bf16[64,32,512]{2,0,1:T(8,128)(2,1)}), bf16[64,32,512]{2,0,1:T(8,128)(2,1)S(1)}, u32[]{:S(2)}, u32[]{:S(2)}) async-start(bf16[64,32,512]{2,0,1:T(8,128)(2,1)} %convert_bitcast_fusion.1), calls=%async_computation.1 | async-start | bytes 4194304 | tf_op jit(solution)/shard_map/all_to_all | solution.py:48
  96.8 153.6 %all-reduce.3.cloned.1.call-start = ((), (), s32[]{:S(2)}) async-start(), calls=%async_computation.6 | async-start | bytes 12582912 | tf_op jit(solution)/shard_map/psum | solution.py:52
  131.2 410.0 %all-reduce.5.cloned.1.call-start = ((), (), s32[]{:S(2)}) async-start(), calls=%async_computation.7 | async-start | bytes 12582912 | tf_op jit(solution)/shard_map/psum | solution.py:52
  311.4 2.1 copy-start
  313.9 64.7 %copy-start.2 = (f32[64,2048]{1,0:T(8,128)}, f32[64,2048]{1,0:T(8,128)S(1)}, u32[]{:S(2)}) copy-start(f32[64,2048]{1,0:T(8,128)S(1)} %get-tuple-element.12) | copy-start | bytes 1572868
  606.7 2.1 copy-start.3
  721.7 2.1 copy-start.1
Sparse Core Ops, SparseCore 0:
  131.3 119.0 all-reduce.2
  422.4 118.6 all-reduce.4
where the time goes:
time: 733 us; the launch traced here: 732 us
  blocking collectives  346 us (47%)
  waiting for transfers between devices  263 us (36%)
  matrix products  38.8 us (5%)
  other arithmetic  35 us (5%)
  local copies, waits for them, and re-layouts  24.4 us (3%)
  between operations  14.3 us (2%)
  starting transfers between devices  10.4 us (1%)
    psum x2, waiting for transfers between devices, adjoint(): total = lax.psum(owned, 'ray')  238 us
    psum x3, blocking collectives, ray_norm(): total = lax.psum(jnp.sum(rays * rays, axis=1), ('ray', 'tile'))  197 us
    all_to_all x3, blocking collectives, fetch(): lax.all_to_all(outgoing, 'tile', split_axis=1, concat_axis=1, tiled=True)  93.6 us
    all_to_all x1, blocking collectives, adjoint(): lax.all_to_all(terms, 'tile', split_axis=1, concat_axis=1, tiled=True)  30.1 us
    all_to_all x1, waiting for transfers between devices, adjoint(): lax.all_to_all(terms, 'tile', split_axis=1, concat_axis=1, tiled=True)  25.1 us
    psum x2, blocking collectives, cell_norm(): total = lax.psum(local, 'tile')  24.9 us
    dot_general x3, matrix products, forward(): jnp.einsum('cnk,nrk->ncr', tiles, sensitivity, preferred_element_type=jnp...  18.1 us
    unnamed x15, local copies, waits for them, and re-layouts  15.1 us
  transfers between devices with their start and end apart: 4, of which 3 were waited for; matrix products, arithmetic and copies ran while one was open for 2% of the time, Pallas kernels for 0%

commit v1 on v0

--- a/solution.py
+++ b/solution.py
@@ -27,7 +27,9 @@
     def fetch(field_bf):
         owned = field_bf.reshape(columns, TILE_DEV, CB)
         outgoing = jnp.take(owned, requests, axis=1)
-        tiles = lax.all_to_all(outgoing, "tile", split_axis=1, concat_axis=1, tiled=True)
+        pieces = jnp.split(outgoing, lax.axis_size("tile"), axis=1)
+        received = lax.all_to_all(jnp.stack(pieces), "tile", 0, 0)
+        tiles = jnp.concatenate(received, axis=1)
         return tiles
 
     def forward(field_bf):

time: 733 us -> 732 us (level)
  blocking collectives: 346 us -> 375 us
  waiting for transfers between devices: 263 us -> 238 us
    all_to_all x1 -> x2, blocking collectives: 30.1 us -> 60 us  [adjoint(): lax.all_to_all(terms, 'tile', split_axis=1, concat_axis=1, tiled=True)]
    all_to_all x1 -> x0, waiting for transfers between devices: 25.1 us -> none  [adjoint(): lax.all_to_all(terms, 'tile', split_axis=1, concat_axis=1, tiled=True)]
    unnamed x15 -> x36, local copies, waits for them, and re-layouts: 15.1 us -> 15.5 us
  transfers between devices with their start and end apart: 4 -> 3, of which waited for: 3 -> 2; matrix products, arithmetic and copies ran while one was open for 2% -> 0% of each run, Pallas kernels for 0% -> 0%
where the time goes in v1:
time: 732 us; the launch traced here: 731 us
  blocking collectives  375 us (51%)
  waiting for transfers between devices  238 us (33%)
  matrix products  37.4 us (5%)
  other arithmetic  35 us (5%)
  local copies, waits for them, and re-layouts  24.8 us (3%)
  between operations  14.5 us (2%)
    psum x2, waiting for transfers between devices, adjoint(): total = lax.psum(owned, 'ray')  238 us
    psum x3, blocking collectives, ray_norm(): total = lax.psum(jnp.sum(rays * rays, axis=1), ('ray', 'tile'))  197 us
    all_to_all x3, blocking collectives, fetch(): received = lax.all_to_all(jnp.stack(pieces), 'tile', 0, 0)  93.6 us
    all_to_all x2, blocking collectives, adjoint(): lax.all_to_all(terms, 'tile', split_axis=1, concat_axis=1, tiled=True)  60 us
    psum x2, blocking collectives, cell_norm(): total = lax.psum(local, 'tile')  24.9 us
    dot_general x3, matrix products, forward(): jnp.einsum('cnk,nrk->ncr', tiles, sensitivity, preferred_element_type=jnp...  18.1 us
    unnamed x36, local copies, waits for them, and re-layouts  15.5 us
  transfers between devices with their start and end apart: 3, of which 2 were waited for; matrix products, arithmetic and copies ran while one was open for 0% of the time, Pallas kernels for 0%

profile of v1, /device:TPU:1, one launch (start us, length us, event | category | flops | bytes accessed | tf_op | source)
XLA Modules:
  0.0 731.4 jit_solution(9402864838073610886)
XLA Ops:
  8.5 6.0 all-to-all-start
  16.5 67.7 %psum.49 = f32[64]{0:T(128)S(1)} all-reduce(f32[64]{0:T(128)S(1)} %multiply_reduce_fusion.4), channel_id=1, replica_groups=mesh['ray'=16,'tile'=8] {'ray','tile'}, use_global_device_ids=true, to_apply=%region_1.0 | all-reduce | flops 64 | bytes 512 | tf_op jit(solution)/shard_map/psum | solution.py:63
  87.4 5.0 convert_bitcast_fusion.1
  92.4 29.9 %all_to_all.30 = bf16[64,32,512]{2,0,1:T(8,128)(2,1)S(1)} all-to-all(bf16[64,32,512]{2,0,1:T(8,128)(2,1)S(1)} %convert_bitcast_fusion.1), channel_id=1, replica_groups=mesh['ray'=16,'tile'=8] {'tile'}, dimensions={1} | all-to-all | bytes 4194304 | tf_op jit(solution)/shard_map/all_to_all | solution.py:50
  124.0 6.3 copy.39
  130.3 119.2 %all-reduce.3.cloned.1.call-done = f32[64,24576]{1,0:T(8,128)} async-done(((f32[64,24576]{1,0:T(8,128)}), f32[64,24576]{1,0:T(8,128)}) %all-reduce.3.cloned.1.call-update) | async-done | bytes 6291472 | tf_op jit(solution)/shard_map/psum | solution.py:54
  249.6 3.3 multiply_reduce_fusion.1
  252.8 12.4 %psum.51 = f32[64]{0:T(128)S(1)} all-reduce(f32[64]{0:T(128)S(1)} %multiply_reduce_fusion.1), channel_id=1, replica_groups=mesh['ray'=16,'tile'=8] {'tile'}, use_global_device_ids=true, to_apply=%region_4.6 | all-reduce | flops 64 | bytes 512 | tf_op jit(solution)/shard_map/psum | solution.py:59
  273.1 31.7 %all_to_all.31 = bf16[8,64,4,512]{3,1,2,0:T(8,128)(2,1)S(1)} all-to-all(bf16[8,64,4,512]{3,1,2,0:T(8,128)(2,1)S(1)} %fusion.35), channel_id=1, replica_groups=mesh['ray'=16,'tile'=8] {'tile'}, dimensions={0} | all-to-all | bytes 4194304 | tf_op jit(solution)/shard_map/all_to_all | solution.py:31
  304.8 6.0 fusion.65
  313.2 64.5 %psum.52 = f32[64]{0:T(128)S(1)} all-reduce(f32[64]{0:T(128)S(1)} %get-tuple-element.11), channel_id=1, replica_groups=mesh['ray'=16,'tile'=8] {'ray','tile'}, use_global_device_ids=true, to_apply=%region_6.0 | all-reduce | flops 64 | bytes 512 | tf_op jit(solution)/shard_map/psum | solution.py:63
  378.6 5.0 convert_bitcast_fusion
  383.6 30.1 %all_to_all.32 = bf16[64,32,512]{2,0,1:T(8,128)(2,1)S(1)} all-to-all(bf16[64,32,512]{2,0,1:T(8,128)(2,1)S(1)} %convert_bitcast_fusion), channel_id=1, replica_groups=mesh['ray'=16,'tile'=8] {'tile'}, dimensions={1} | all-to-all | bytes 4194304 | tf_op jit(solution)/shard_map/all_to_all | solution.py:50
  415.4 6.3 copy.41
  421.7 118.9 %all-reduce.5.cloned.1.call-done = f32[64,24576]{1,0:T(8,128)} async-done(((f32[64,24576]{1,0:T(8,128)}), f32[64,24576]{1,0:T(8,128)}) %all-reduce.5.cloned.1.call-update) | async-done | bytes 6291472 | tf_op jit(solution)/shard_map/psum | solution.py:54
  540.6 5.8 multiply_reduce_fusion
  546.3 12.4 %psum.54 = f32[64]{0:T(128)S(1)} all-reduce(f32[64]{0:T(128)S(1)} %multiply_reduce_fusion), channel_id=1, replica_groups=mesh['ray'=16,'tile'=8] {'tile'}, use_global_device_ids=true, to_apply=%region_9.12 | all-reduce | flops 64 | bytes 512 | tf_op jit(solution)/shard_map/psum | solution.py:59
  558.8 5.2 fusion.10
  568.5 31.7 %all_to_all.33 = bf16[8,64,4,512]{3,1,2,0:T(8,128)(2,1)S(1)} all-to-all(bf16[8,64,4,512]{3,1,2,0:T(8,128)(2,1)S(1)} %fusion.27), channel_id=1, replica_groups=mesh['ray'=16,'tile'=8] {'tile'}, dimensions={0} | all-to-all | bytes 4194304 | tf_op jit(solution)/shard_map/all_to_all | solution.py:31
  600.3 6.0 fusion.66
  608.7 64.8 %psum.55 = f32[64]{0:T(128)S(1)} all-reduce(f32[64]{0:T(128)S(1)} %multiply_reduce_fusion.2), channel_id=1, replica_groups=mesh['ray'=16,'tile'=8] {'ray','tile'}, use_global_device_ids=true, to_apply=%region_11.14 | all-reduce | flops 64 | bytes 512 | tf_op jit(solution)/shard_map/psum | solution.py:63
  673.5 7.4 %fusion.62 = (bf16[64,24576]{1,0:T(8,128)(2,1)S(1)}, f32[64,24576]{1,0:T(8,128)}) fusion(f32[64]{0:T(128)S(1)} %multiply_divide_fusion, f32[64]{0:T(128)S(1)} %add_sqrt_fusion, f32[64,24576]{1,0:T(8,128)} %all-reduce.5.cloned.1.call-done, f32[64]{0:T(128)S(1)} %get-tuple-element.13, f32[64]{0:T(128)S(1)} %get-tuple-element.9, ...), kind=kLoop, calls=%fused_computation.124 | loop fusion | flops 15728640 | bytes 22021632 | tf_op jit(solution)/shard_map/convert_element_type | solution.py:93
  685.4 30.1 %all_to_all.34 = bf16[8,64,4,512]{3,1,2,0:T(8,128)(2,1)S(1)} all-to-all(bf16[8,64,4,512]{3,1,2,0:T(8,128)(2,1)S(1)} %fusion.19), channel_id=1, replica_groups=mesh['ray'=16,'tile'=8] {'tile'}, dimensions={0} | all-to-all | bytes 4194304 | tf_op jit(solution)/shard_map/all_to_all | solution.py:31
  715.5 6.0 fusion.67
  (82 shorter events, 35.1 us)
Async XLA Ops:
  8.5 76.9 %all-to-all-start = ((s32[1,8,4]{2,0,1:T(1,128)}), s32[1,8,4]{2,0,1:T(1,128)S(1)}, u32[]{:S(2)}, u32[]{:S(2)}) async-start(s32[1,8,4]{2,0,1:T(1,128)} %copy.22), calls=%async_computation | async-start | bytes 8192 | tf_op jit(solution)/shard_map/all_to_all | solution.py:17
  14.5 235.1 %all-reduce.3.cloned.1.call-start = ((), (), s32[]{:S(2)}) async-start(), calls=%async_computation.6 | async-start | bytes 12582912 | tf_op jit(solution)/shard_map/psum | solution.py:54
  130.3 410.3 %all-reduce.5.cloned.1.call-start = ((), (), s32[]{:S(2)}) async-start(), calls=%async_computation.7 | async-start | bytes 12582912 | tf_op jit(solution)/shard_map/psum | solution.py:54
  310.8 2.1 copy-start
  313.2 64.7 %copy-start.2 = (f32[64,2048]{1,0:T(8,128)}, f32[64,2048]{1,0:T(8,128)S(1)}, u32[]{:S(2)}) copy-start(f32[64,2048]{1,0:T(8,128)S(1)} %get-tuple-element.12) | copy-start | bytes 1572868
  606.3 2.1 copy-start.3
  721.6 2.1 copy-start.1
Sparse Core Ops, SparseCore 0:
  130.4 119.1 all-reduce.2
  421.8 118.6 all-reduce.4
